TPU v7x, 32 devices: a whole 2x2x4 slice. The times are simulated.
32 devices in a mesh: groups: 2 (over x), tensor: 16 (over z, y, core).
Axes of the slice: x: 2, y: 2, z: 4, core: 2. Of those that a mesh axis runs over, the one named last changes fastest.
Arguments:
- tokens: bfloat16 [1024, 8192], P('groups', 'tensor'), parts along dimension 0, may hold values from -6 to 6
- norm_gain: float32 [8192], P('tensor'), may hold values from 0.1 to 1.9
- w_in: bfloat16 [8192, 3, 8192], P(None, None, 'tensor'), may hold values from -0.0625 to 0.0625
- w_short: float32 [3, 3, 8192], P(None, None, 'tensor'), may hold values from -3 to 3
- filters: bfloat16 [512, 128], P('tensor'), may hold values from -0.5 to 0.5
- skip: float32 [8192], P('tensor'), may hold values from -4 to 4
- w_out: bfloat16 [8192, 8192], P('tensor'), may hold values from -0.0625 to 0.0625
Outputs:
- mixed: bfloat16 [1024, 8192], P('groups', 'tensor'), parts along dimension 0
There are 2 independent parts, one for each index of `groups`. A program takes and returns all parts, laid end to end along the dimension named above; an argument that names none is the same for every part. Nothing has to cross between parts.
All inputs are finite; a program needn't handle non-finite values.
Results may differ from a plain program's by a relative error of at most 0.0085.
Values may be sent and summed in bfloat16 or wider, within the bound.
A program may use at most 192 MiB of HBM per device.

v0:
```python
import jax
import jax.numpy as jnp
from jax import lax
from jax.sharding import PartitionSpec as P

D = 8192


def shifted(field, lag):
    pads = ((lag, 0),) + ((0, 0),) * (field.ndim - 1)
    return jnp.pad(field, pads)[: field.shape[0]]


def lag_matrix(filters, rows):
    count, taps = filters.shape
    length = taps + rows
    line = jnp.concatenate([filters, jnp.zeros((count, rows), filters.dtype)], axis=1)
    tiled = jnp.tile(line, (1, rows))[:, : rows * (length - 1)]
    return tiled.reshape(count, rows, length - 1)[:, :, :rows]


def on_device(tokens, norm_gain, w_in, w_short, filters, skip, w_out):
    wide = tokens.astype(jnp.float32)
    squares = lax.psum(jnp.sum(wide * wide, axis=1, keepdims=True), "tensor")
    factor = lax.rsqrt(squares / D + 1e-05)
    normed = (wide * factor * norm_gain[None, :]).astype(jnp.bfloat16)
    width = w_in.shape[0]
    local = w_in.shape[2]
    rows = tokens.shape[0]
    w_flat = w_in.reshape(width, 3 * local)
    chosen = w_flat
    proj = jnp.dot(
        lax.all_gather(normed, "tensor", axis=1, tiled=True),
        chosen,
        preferred_element_type=jnp.float32,
    )
    proj = proj.reshape(rows, 3, local)
    short = w_short[0][None] * proj
    for lag in range(1, w_short.shape[0]):
        short = short + w_short[lag][None] * shifted(proj, lag)
    gated = (short[:, 1] * short[:, 2]).astype(jnp.bfloat16)
    count = filters.shape[0]
    lagged = lag_matrix(filters, rows)
    grouped = gated.reshape(rows, count, local // count)
    conv = jnp.einsum("fst,sfg->tfg", lagged, grouped, preferred_element_type=jnp.float32)
    conv = conv.reshape(rows, local)
    hidden = ((conv + skip[None, :] * gated.astype(jnp.float32)) * short[:, 0]).astype(jnp.bfloat16)
    w_cols = lax.all_to_all(w_out, "tensor", split_axis=1, concat_axis=0, tiled=True)
    chosen = w_cols
    summed = jnp.dot(
        lax.all_gather(hidden, "tensor", axis=1, tiled=True),
        chosen,
        preferred_element_type=jnp.float32,
    )
    return (wide + summed).astype(jnp.bfloat16)


def solution(mesh):
    return jax.shard_map(
        on_device,
        mesh=mesh,
        in_specs=(
            P("groups", "tensor"),
            P("tensor"),
            P(None, None, "tensor"),
            P(None, None, "tensor"),
            P("tensor", None),
            P("tensor"),
            P("tensor", None),
        ),
        out_specs=P("groups", "tensor"),
        check_vma=False,
    )
```

profile of v0, /device:TPU:0, one launch (start us, length us, event | category | flops | bytes accessed | tf_op | source)
XLA Modules:
  0.0 382.3 jit_solution(3870038537014596827)
XLA Ops:
  6.5 0.0 all-gather.3.cloned.1.call-start
  6.5 1.2 fusion.10
  7.8 35.0 %psum.7 = f32[512,1]{0,1:T(1,128)S(1)} all-reduce(f32[512,1]{0,1:T(1,128)S(1)} %bitcast.46), channel_id=1, replica_groups=mesh['groups'=2,'tensor'=16] {'tensor'}, use_global_device_ids=true, to_apply=%region_1.0 | all-reduce | flops 512 | bytes 4096 | tf_op jit(solution)/shard_map/psum | solution.py:24
  42.7 2.0 fusion.12
  44.7 0.0 all-gather.3.cloned.1.call-update
  44.8 12.1 %copy.16 = bf16[512,8192]{0,1:T(8,128)(2,1)} copy(bf16[512,8192]{1,0:T(8,128)(2,1)} %param.13) | data formatting | bytes 16777216 | tf_op args[6]
  56.8 4.8 %all-to-all-start = ((bf16[512,16,512]{0,2,1:T(8,128)(2,1)}), bf16[512,16,512]{0,2,1:T(8,128)(2,1)}, u32[]{:S(2)}, u32[]{:S(2)}) async-start(bf16[512,16,512]{0,2,1:T(8,128)(2,1)} %bitcast.41), calls=%async_computation | async-start | bytes 16777216 | tf_op jit(solution)/shard_map/all_to_all | solution.py:48
  61.6 0.0 copy-start.2
  61.6 0.0 all-gather.5.cloned.1.call-start
  61.7 33.5 %copy.13 = bf16[8192,3,512]{0,2,1:T(8,128)(2,1)} copy(bf16[8192,3,512]{2,0,1:T(8,128)(2,1)} %param.9) | data formatting | bytes 50331648 | tf_op args[2]
  95.1 0.0 copy-done.2
  95.1 2.9 tile.4
  98.0 67.1 %copy.18 = bf16[4,8,512,640]{3,1,2,0:T(8,128)(2,1)S(1)} copy(bf16[4,8,512,640]{3,2,1,0:T(8,128)(2,1)S(1)} %bitcast.39) | data formatting | bytes 41943040
  165.1 8.1 %slice.42 = bf16[32,327168]{1,0:T(8,128)(2,1)} slice(bf16[32,327680]{1,0:T(8,128)(2,1)S(1)} %bitcast.40), slice={[0:32], [0:327168]} | slice | bytes 41877504 | tf_op jit(solution)/shard_map/slice | solution.py:18
  173.2 0.0 copy-start.1
  173.2 69.0 %reshape.30 = bf16[32,512,639]{2,1,0:T(8,128)(2,1)} reshape(bf16[32,327168]{1,0:T(8,128)(2,1)} %slice.42) | data formatting | bytes 41877504 | tf_op jit(solution)/shard_map/reshape | solution.py:19
  242.2 0.0 copy-done.1
  242.3 0.0 all-gather.3.cloned.1.call-done
  242.3 19.6 %fusion = f32[512,3,512]{2,0,1:T(8,128)S(1)} fusion(bf16[8192,3,512]{0,2,1:T(8,128)(2,1)} %copy.13, bf16[512,8192]{1,0:T(8,128)(2,1)} %all-gather.3.cloned.1.call-done), kind=kOutput, calls=%fused_computation | convolution fusion | flops 12884901888 | bytes 36700160 | tf_op jit(solution)/shard_map/dot_general | solution.py:32
  261.9 0.9 fusion.7
  262.8 0.9 fusion.15
  263.8 2.1 copy.14
  265.9 0.0 copy-start.3
  265.9 9.2 %fusion.2 = f32[32,16,512]{2,1,0:T(8,128)} fusion(bf16[512,32,16]{0,2,1:T(8,128)(2,1)} %bitcast.44, bf16[32,512,639]{2,1,0:T(8,128)(2,1)} %reshape.30), kind=kOutput, calls=%fused_computation.2 | convolution fusion | flops 268435456 | bytes 18350080 | tf_op jit(solution)/shard_map/fst,sfg->tfg/dot_general | solution.py:45
  275.1 2.6 copy.15
  277.6 0.0 copy-done.3
  277.7 2.5 fusion.14
  280.2 0.0 all-gather.5.cloned.1.call-update
  280.2 0.0 all-to-all-done
  280.2 0.0 copy-start
  280.2 12.4 %copy.17 = bf16[16,512,512]{2,1,0:T(8,128)(2,1)} copy(bf16[16,512,512]{1,2,0:T(8,128)(2,1)} %bitcast.15) | data formatting | bytes 16777216 | tf_op jit(solution)/shard_map/all_to_all | solution.py:48
  292.6 71.8 %all-gather.5.cloned.1.call-done = bf16[512,8192]{1,0:T(8,128)(2,1)} async-done(((bf16[512,512]{1,0:T(8,128)(2,1)}), bf16[512,8192]{1,0:T(8,128)(2,1)}) %all-gather.5.cloned.1.call-update) | async-done | bytes 8388624 | tf_op jit(solution)/shard_map/all_gather | solution.py:51
  364.4 0.0 copy-done
  364.4 11.0 %fusion.9 = bf16[512,512]{1,0:T(8,128)(2,1)} fusion(bf16[512,8192]{1,0:T(8,128)(2,1)} %all-gather.5.cloned.1.call-done, bf16[8192,512]{1,0:T(8,128)(2,1)} %bitcast.43, bf16[512,512]{1,0:T(8,128)(2,1)S(1)} %copy-done), kind=kOutput, calls=%fused_computation.14 | convolution fusion | flops 4295753728 | bytes 17825792 | tf_op jit(solution)/shard_map/dot_general | solution.py:50
  (3 shorter events, 0.0 us)
Async XLA Ops:
  6.5 235.7 %all-gather.3.cloned.1.call-start = ((), (), s32[]{:S(2)}) async-start(), calls=%async_computation.1 | async-start | bytes 8912896 | tf_op jit(solution)/shard_map/all_gather | solution.py:33
  56.8 223.4 %all-to-all-start = ((bf16[512,16,512]{0,2,1:T(8,128)(2,1)}), bf16[512,16,512]{0,2,1:T(8,128)(2,1)}, u32[]{:S(2)}, u32[]{:S(2)}) async-start(bf16[512,16,512]{0,2,1:T(8,128)(2,1)} %bitcast.41), calls=%async_computation | async-start | bytes 16777216 | tf_op jit(solution)/shard_map/all_to_all | solution.py:48
  61.6 33.5 %copy-start.2 = (bf16[32,128]{1,0:T(8,128)(2,1)S(1)}, bf16[32,128]{1,0:T(8,128)(2,1)}, u32[]{:S(2)}) copy-start(bf16[32,128]{1,0:T(8,128)(2,1)} %param.11) | copy-start | bytes 24580
  61.6 302.8 %all-gather.5.cloned.1.call-start = ((), (), s32[]{:S(2)}) async-start(), calls=%async_computation.2 | async-start | bytes 8912896 | tf_op jit(solution)/shard_map/all_gather | solution.py:51
  173.2 69.0 %copy-start.1 = (f32[3,3,512]{2,1,0:T(4,128)S(1)}, f32[3,3,512]{2,1,0:T(4,128)}, u32[]{:S(2)}) copy-start(f32[3,3,512]{2,1,0:T(4,128)} %param.10) | copy-start | bytes 55300
  265.9 11.8 %copy-start.3 = (f32[512]{0:T(512)S(1)}, f32[512]{0:T(512)}, u32[]{:S(2)}) copy-start(f32[512]{0:T(512)} %param.12) | copy-start | bytes 6148
  280.2 84.2 %copy-start = (bf16[512,512]{1,0:T(8,128)(2,1)S(1)}, bf16[512,512]{1,0:T(8,128)(2,1)}, u32[]{:S(2)}) copy-start(bf16[512,512]{1,0:T(8,128)(2,1)} %param.7) | copy-start | bytes 1572868
Sparse Core Ops, SparseCore 0:
  44.9 189.7 all-gather.2
  280.3 84.0 all-gather.4
where the time goes:
time: 384 us; the launch traced here: 382 us
  local copies, waits for them, and re-layouts  210 us (55%)
  waiting for transfers between devices  71.8 us (19%)
  matrix products  39.9 us (10%)
  blocking collectives  35 us (9%)
  between operations  13.5 us (4%)
  other arithmetic  7.65 us (2%)
  starting transfers between devices  4.8 us (1%)
    unnamed x11, local copies, waits for them, and re-layouts  113 us
    all_gather x1, waiting for transfers between devices, on_device(): lax.all_gather(hidden, 'tensor', axis=1, tiled=True)  71.8 us
    reshape x1, local copies, waits for them, and re-layouts, lag_matrix(): return tiled.reshape(count, rows, length - 1)[:, :, :rows]  69 us
    psum x1, blocking collectives, on_device(): squares = lax.psum(jnp.sum(wide * wide, axis=1, keepdims=True), 'tensor')  35 us
    dot_general x1, matrix products, on_device(): jnp.dot(lax.all_gather(normed, 'tensor', axis=1, tiled=True), chosen, pre...  19.6 us
    all_to_all x1, local copies, waits for them, and re-layouts, on_device(): lax.all_to_all(w_out, 'tensor', split_axis=1, concat_axis=0, tiled=True)  12.4 us
    dot_general x1, matrix products, on_device(): jnp.dot(lax.all_gather(hidden, 'tensor', axis=1, tiled=True), chosen, pre...  11 us
    dot_general x1, matrix products, on_device(): jnp.einsum('fst,sfg->tfg', lagged, grouped, preferred_element_type=jnp.fl...  9.22 us
  transfers between devices with their start and end apart: 3, of which 1 were waited for; matrix products, arithmetic and copies ran while one was open for 64% of the time, Pallas kernels for 0%

commit v1 on v0

v1 whole, which is shorter than its diff:
```python
import jax
import jax.numpy as jnp
from jax import lax
from jax.sharding import PartitionSpec as P

D = 8192


def shifted(field, lag):
    pads = ((lag, 0),) + ((0, 0),) * (field.ndim - 1)
    return jnp.pad(field, pads)[: field.shape[0]]


def lag_block(filters, block):
    count, taps = filters.shape
    rows = 2 * block
    length = taps + rows
    line = jnp.concatenate([filters, jnp.zeros((count, rows), filters.dtype)], axis=1)
    tiled = jnp.tile(line, (1, rows))[:, : rows * (length - 1)]
    return tiled.reshape(count, rows, length - 1)[:, :, block:rows]


def on_device(tokens, norm_gain, w_in, w_short, filters, skip, w_out):
    wide = tokens.astype(jnp.float32)
    squares = lax.psum(jnp.sum(wide * wide, axis=1, keepdims=True), "tensor")
    factor = lax.rsqrt(squares / D + 1e-05)
    scaled = (wide * norm_gain[None, :]).astype(jnp.bfloat16)
    local = w_in.shape[2]
    rows = tokens.shape[0]
    x = lax.all_gather(scaled, "tensor", axis=1, tiled=True)
    short = []
    for b in range(3):
        proj = jnp.dot(x, w_in[:, b], preferred_element_type=jnp.float32) * factor
        out = w_short[0, b][None] * proj
        for lag in range(1, w_short.shape[0]):
            out = out + w_short[lag, b][None] * shifted(proj, lag)
        short.append(out)
    q, k, v = short
    gated = (k * v).astype(jnp.bfloat16)
    count, taps = filters.shape
    group = local // count
    blocks = rows // taps
    lagged = lag_block(filters, taps)
    cells = gated.T.reshape(count, group, blocks, taps)
    before = jnp.pad(cells, ((0, 0), (0, 0), (1, 0), (0, 0)))[:, :, :blocks]
    pair = jnp.concatenate([before, cells], axis=3).reshape(count, group * blocks, 2 * taps)
    conv = jnp.einsum("fms,fst->fmt", pair, lagged, preferred_element_type=jnp.float32)
    conv = conv.reshape(local, rows).T
    hidden = ((conv + skip[None, :] * gated.astype(jnp.float32)) * q).astype(jnp.bfloat16)
    part = jnp.dot(hidden, w_out, preferred_element_type=jnp.float32).astype(jnp.bfloat16)
    summed = lax.psum_scatter(part, "tensor", scatter_dimension=1, tiled=True)
    return (wide + summed.astype(jnp.float32)).astype(jnp.bfloat16)


def solution(mesh):
    return jax.shard_map(
        on_device,
        mesh=mesh,
        in_specs=(
            P("groups", "tensor"),
            P("tensor"),
            P(None, None, "tensor"),
            P(None, None, "tensor"),
            P("tensor", None),
            P("tensor"),
            P("tensor", None),
        ),
        out_specs=P("groups", "tensor"),
        check_vma=False,
    )
```

time: 384 us -> 244 us (0.64)
  local copies, waits for them, and re-layouts: 210 us -> 28 us
  waiting for transfers between devices: 71.8 us -> 121 us
  starting transfers between devices: 4.8 us -> 0.04 us
    unnamed x11 -> x9, local copies, waits for them, and re-layouts: 113 us -> 3.85 us
    reduce_scatter x0 -> x1, waiting for transfers between devices: none -> 102 us  [on_device(): summed = lax.psum_scatter(part, 'tensor', scatter_dimension=1, tiled=True)]
    all_gather x2 -> x1, waiting for transfers between devices: 71.8 us -> 18.6 us  [on_device(): x = lax.all_gather(scaled, 'tensor', axis=1, tiled=True)]
    reshape x2 -> x4, local copies, waits for them, and re-layouts: 71.6 us -> 19 us  [the longest x1 18.4 us: lag_block(): return tiled.reshape(count, rows, length - 1)[:, :, block:rows]]
    all_to_all x1 -> x0, local copies, waits for them, and re-layouts: 12.4 us -> none  [on_device(): lax.all_to_all(w_out, 'tensor', split_axis=1, concat_axis=0, tiled=True)]
    slice x1 -> x3, local copies, waits for them, and re-layouts: 8.08 us -> 3.32 us  [the longest x1 2.96 us: lag_block(): tiled = jnp.tile(line, (1, rows))[:, :rows * (length - 1)]]
    all_to_all x1 -> x0, starting transfers between devices: 4.76 us -> none  [on_device(): lax.all_to_all(w_out, 'tensor', split_axis=1, concat_axis=0, tiled=True)]
    dot_general x3 -> x5, matrix products: 39.9 us -> 39.7 us  [the longest x3 27.2 us: on_device(): proj = jnp.dot(x, w_in[:, b], preferred_element_type=jnp.float32) * factor]
  transfers between devices with their start and end apart: 3 -> 2, of which waited for: 1 -> 2; matrix products, arithmetic and copies ran while one was open for 64% -> 11% of each run, Pallas kernels for 0% -> 0%
where the time goes in v1:
time: 244 us; the launch traced here: 243 us
  waiting for transfers between devices  121 us (50%)
  matrix products  39.7 us (16%)
  blocking collectives  36.7 us (15%)
  local copies, waits for them, and re-layouts  28 us (11%)
  between operations  13.5 us (6%)
  other arithmetic  4.63 us (2%)
    reduce_scatter x1, waiting for transfers between devices, on_device(): summed = lax.psum_scatter(part, 'tensor', scatter_dimension=1, tiled=True)  102 us
    psum x1, blocking collectives, on_device(): squares = lax.psum(jnp.sum(wide * wide, axis=1, keepdims=True), 'tensor')  36.7 us
    dot_general x3, matrix products, on_device(): proj = jnp.dot(x, w_in[:, b], preferred_element_type=jnp.float32) * factor  27.2 us
    all_gather x1, waiting for transfers between devices, on_device(): x = lax.all_gather(scaled, 'tensor', axis=1, tiled=True)  18.6 us
    reshape x1, local copies, waits for them, and re-layouts, lag_block(): return tiled.reshape(count, rows, length - 1)[:, :, block:rows]  18.4 us
    dot_general x1, matrix products, on_device(): jnp.dot(hidden, w_out, preferred_element_type=jnp.float32)  10.4 us
  transfers between devices with their start and end apart: 2, of which 2 were waited for; matrix products, arithmetic and copies ran while one was open for 11% of the time, Pallas kernels for 0%

profile of v1, /device:TPU:0, one launch (start us, length us, event | category | flops | bytes accessed | tf_op | source)
XLA Modules:
  0.0 243.2 jit_solution(13564471336237378709)
XLA Ops:
  6.5 0.0 all-gather.2.cloned.1.call-start
  6.5 2.0 fusion.37
  8.5 0.0 all-gather.2.cloned.1.call-update
  8.5 0.0 reduce-scatter.2.cloned.1.call-start
  8.6 0.7 concatenate.14
  9.3 0.5 tile.4
  9.9 3.8 %copy.12 = bf16[4,8,256,384]{3,1,2,0:T(8,128)(2,1)S(1)} copy(bf16[4,8,256,384]{3,2,1,0:T(8,128)(2,1)S(1)} %bitcast.39) | data formatting | bytes 12582912
  13.7 3.0 %slice.84 = bf16[32,98048]{1,0:T(8,128)(2,1)} slice(bf16[32,98304]{1,0:T(8,128)(2,1)S(1)} %bitcast.40), slice={[0:32], [0:98048]} | slice | bytes 12550144 | tf_op jit(solution)/shard_map/slice | solution.py:19
  16.7 0.0 copy-start.1
  16.7 18.4 %reshape.29 = bf16[32,256,383]{2,1,0:T(8,128)(2,1)} reshape(bf16[32,98048]{1,0:T(8,128)(2,1)} %slice.84) | data formatting | bytes 12550144 | tf_op jit(solution)/shard_map/reshape | solution.py:20
  35.0 36.7 %psum.7 = f32[512,1]{0,1:T(1,128)S(1)} all-reduce(f32[512,1]{0,1:T(1,128)S(1)} %bitcast.49), channel_id=1, replica_groups=mesh['groups'=2,'tensor'=16] {'tensor'}, use_global_device_ids=true, to_apply=%region_1.0 | all-reduce | flops 512 | bytes 4096 | tf_op jit(solution)/shard_map/psum | solution.py:25
  71.7 0.0 copy-done.1
  71.8 18.6 %all-gather.2.cloned.1.call-done = bf16[512,8192]{1,0:T(8,128)(2,1)} async-done(((bf16[512,512]{1,0:T(8,128)(2,1)}), bf16[512,8192]{1,0:T(8,128)(2,1)}) %all-gather.2.cloned.1.call-update) | async-done | bytes 8388624 | tf_op jit(solution)/shard_map/all_gather | solution.py:30
  90.4 0.0 copy-start.2
  90.4 10.5 %fusion.14 = f32[512,512]{1,0:T(8,128)S(1)} fusion(bf16[512,8192]{1,0:T(8,128)(2,1)} %all-gather.2.cloned.1.call-done, bf16[8192,3,512]{2,0,1:T(8,128)(2,1)} %param.9, f32[512]{0:T(512)S(1)} %bitcast.53), kind=kOutput, calls=%fused_computation.16 | convolution fusion | flops 4295229440 | bytes 17827840 | tf_op jit(solution)/shard_map/dot_general | solution.py:33
  101.0 0.0 copy-done.2
  101.0 7.1 %fusion.11 = f32[512,512]{1,0:T(8,128)S(1)} fusion(bf16[512,8192]{1,0:T(8,128)(2,1)S(1)} %copy-done.2, bf16[8192,3,512]{2,0,1:T(8,128)(2,1)} %param.9, f32[512]{0:T(512)S(1)} %bitcast.54), kind=kOutput, calls=%fused_computation.15 | convolution fusion | flops 4295229440 | bytes 17827840 | tf_op jit(solution)/shard_map/dot_general | solution.py:33
  108.1 0.7 fusion.24
  108.8 0.2 copy.9
  109.0 0.3 concatenate.12
  109.3 0.1 reshape.28
  109.4 0.3 pad_slice_fusion.6
  109.8 2.1 fusion.9
  111.9 0.2 reshape.30
  112.0 0.3 copy.11
  112.4 0.0 copy-start.3
  112.4 9.6 %fusion.17 = f32[512,512]{1,0:T(8,128)S(1)} fusion(bf16[512,8192]{1,0:T(8,128)(2,1)} %all-gather.2.cloned.1.call-done, bf16[8192,3,512]{2,0,1:T(8,128)(2,1)} %param.9, f32[512]{0:T(512)S(1)} %bitcast.55), kind=kOutput, calls=%fused_computation.17 | convolution fusion | flops 4295229440 | bytes 17827840 | tf_op jit(solution)/shard_map/dot_general | solution.py:33
  122.0 0.0 copy-done.3
  122.0 10.4 %convolution_convert_fusion = bf16[512,8192]{1,0:T(8,128)(2,1)} fusion(bf16[512,8192]{1,0:T(8,128)(2,1)} %param.13, f32[512,512]{1,0:T(8,128)S(1)} %fusion.17, f32[512,512]{0,1:T(8,128)S(1)} %copy.11, bf16[512,512]{1,0:T(8,128)(2,1)S(1)} %fusion.24, f32[512]{0:T(512)S(1)} %bitcast.51, f32[512]{0:T(512)S(1)} %bitcast.52, f32[512]{0:T(512)S(1)} %bitcast.50, ...), kind=kOutput, calls=%fused_computation | convolution fusion | flops 4301783040 | bytes 19406848 | tf_op jit(solution)/shard_map/dot_general | solution.py:50
  132.4 0.0 copy-start
  132.4 0.0 reduce-scatter.2.cloned.1.call-update
  132.4 102.0 %reduce-scatter.2.cloned.1.call-done = bf16[512,512]{1,0:T(8,128)(2,1)} async-done(((bf16[512,8192]{1,0:T(8,128)(2,1)}), bf16[512,512]{1,0:T(8,128)(2,1)}) %reduce-scatter.2.cloned.1.call-update) | async-done | bytes 524304 | tf_op jit(solution)/shard_map/reduce_scatter | solution.py:51
  234.4 0.0 copy-done
  234.4 2.0 fusion.38
  (2 shorter events, 0.0 us)
Async XLA Ops:
  6.5 83.9 %all-gather.2.cloned.1.call-start = ((), (), s32[]{:S(2)}) async-start(), calls=%async_computation.1 | async-start | bytes 8912896 | tf_op jit(solution)/shard_map/all_gather | solution.py:30
  8.5 225.9 %reduce-scatter.2.cloned.1.call-start = ((), (), s32[]{:S(2)}) async-start(), calls=%async_computation.2 | async-start | bytes 8912896 | tf_op jit(solution)/shard_map/reduce_scatter | solution.py:51
  16.7 55.1 %copy-start.1 = (f32[3,3,512]{2,1,0:T(4,128)S(1)}, f32[3,3,512]{2,1,0:T(4,128)}, u32[]{:S(2)}) copy-start(f32[3,3,512]{2,1,0:T(4,128)} %param.10) | copy-start | bytes 55300
  90.4 10.6 %copy-start.2 = (bf16[512,8192]{1,0:T(8,128)(2,1)S(1)}, bf16[512,8192]{1,0:T(8,128)(2,1)}, u32[]{:S(2)}) copy-start(bf16[512,8192]{1,0:T(8,128)(2,1)} %all-gather.2.cloned.1.call-done) | copy-start | bytes 25165828
  112.4 9.6 %copy-start.3 = (f32[512]{0:T(512)S(1)}, f32[512]{0:T(512)}, u32[]{:S(2)}) copy-start(f32[512]{0:T(512)} %param.12) | copy-start | bytes 6148
  132.4 102.0 %copy-start = (bf16[512,512]{1,0:T(8,128)(2,1)S(1)}, bf16[512,512]{1,0:T(8,128)(2,1)}, u32[]{:S(2)}) copy-start(bf16[512,512]{1,0:T(8,128)(2,1)} %param.7) | copy-start | bytes 1572868
Sparse Core Ops, SparseCore 0:
  9.5 80.8 all-gather.1
  132.5 101.8 reduce-scatter.1
